TPU v7x, 128 devices: a whole 4x4x4 slice. The times are simulated.
128 devices in a mesh: dev: 32 (over z, x, core), rep: 4 (over y).
Axes of the slice: x: 4, y: 4, z: 4, core: 2. Of those that a mesh axis runs over, the one named last changes fastest.
Arguments:
- emb_table: float32 [131072, 160], P('dev'), may hold values from -6 to 6
- feature_ids: int32 [16384, 4, 8], P(('dev', 'rep')), may hold values from 0 to 32767
- lengths: int32 [16384, 4], P(('dev', 'rep')), may hold values from 1 to 8
- cotangent: float32 [16384, 4, 160], P(('dev', 'rep')), may hold values from -6 to 6
Outputs:
- pooled: float32 [16384, 4, 160], P(('dev', 'rep'))
- row_grads: float32 [131072, 160], P(('dev', 'rep'))
All inputs are finite; a program needn't handle non-finite values.
Results may differ from a plain program's by a relative error of at most 0.00008.
Values sent between devices are 32-bit elements; how exact they have to be, the bound alone decides.
No kernel may reach another device: no remote copies, remote signals or barrier semaphores. Data moves between devices by JAX's collectives and lax.ppermute only.
A program may use at most 128 MiB of HBM per device.

v0:
```python
import math

import jax
import jax.numpy as jnp
from jax import lax
from jax.sharding import PartitionSpec as P


def laid_out(pieces, dim):
    pieces = jnp.moveaxis(pieces, 0, dim)
    shape = pieces.shape
    return pieces.reshape(*shape[:dim], shape[dim] * shape[dim + 1], *shape[dim + 2 :])


def from_everyone(x, axis):
    copies = jnp.broadcast_to(x, (lax.axis_size(axis), *x.shape))
    return lax.all_to_all(copies, axis, split_axis=0, concat_axis=0, tiled=True)


def gather_directly(x, axis, dim):
    return laid_out(from_everyone(x, axis), dim)


def cut_along(x, dim, length):
    shape = x.shape
    pieces = x.reshape(*shape[:dim], length, shape[dim] // length, *shape[dim + 1 :])
    return jnp.moveaxis(pieces, dim, 0)


def summed_on_arrival(x, axis, dim):
    length = lax.axis_size(axis)
    pieces = lax.all_to_all(cut_along(x, dim, length), axis, 0, 0, tiled=True)
    return jnp.sum(pieces, axis=0)


def relative_ids(id_rows, base_row):
    live_count = jnp.sum((id_rows >= 0).astype(jnp.float32), axis=1)
    share = 1.0 / live_count
    shifted = jnp.where(id_rows >= 0, id_rows - base_row, -1)
    return (shifted, share)


def count_block(shifted, first_col, block_rows):
    columns = first_col + lax.broadcasted_iota(jnp.int32, (1, block_rows), 1)
    result = jnp.zeros((shifted.shape[0], block_rows), jnp.float32)
    for slot in range(shifted.shape[1]):
        result = result + (shifted[:, slot : slot + 1] == columns).astype(jnp.float32)
    return result


def pool_rows(shifted, share, table_rows):
    block_rows = math.gcd(table_rows.shape[0], 1024)
    block_count = table_rows.shape[0] // block_rows

    def add_block(block_index, partial_value):
        table_block = lax.dynamic_slice_in_dim(table_rows, block_index * block_rows, block_rows, 0)
        counts = count_block(shifted, block_index * block_rows, block_rows)
        return partial_value + jnp.dot(
            counts, table_block, precision=lax.Precision.HIGHEST, preferred_element_type=jnp.float32
        )

    start_pool = jnp.zeros((shifted.shape[0], table_rows.shape[1]), jnp.float32)
    summed = lax.fori_loop(0, block_count, add_block, start_pool)
    return summed * share[:, None]


def grad_rows(shifted, scaled, rows_dev):
    block_rows = math.gcd(rows_dev, 1024)
    block_count = rows_dev // block_rows

    def block_grad(block_index):
        counts = count_block(shifted, block_index * block_rows, block_rows)
        return jnp.dot(
            counts.T, scaled, precision=lax.Precision.HIGHEST, preferred_element_type=jnp.float32
        )

    blocks = lax.map(block_grad, jnp.arange(block_count, dtype=jnp.int32))
    return blocks.reshape(rows_dev, scaled.shape[1])


def body(emb_table, feature_ids, lengths, cotangent):
    dev_count = lax.axis_size("dev")
    rows_dev, emb_width = emb_table.shape
    examples, features, bag_len = feature_ids.shape
    owners_each = dev_count // features
    own_index = lax.axis_index("dev")
    own_feature = own_index // owners_each
    base_row = own_index % owners_each * rows_dev
    slot_index = lax.broadcasted_iota(jnp.int32, feature_ids.shape, 2)
    masked = jnp.where(slot_index < lengths[:, :, None], feature_ids, -1)
    all_ids = gather_directly(masked, "dev", 0)
    id_block = all_ids
    own_ids = lax.dynamic_index_in_dim(id_block, own_feature, 1, keepdims=False)
    shifted, share = relative_ids(own_ids, base_row)
    partial_value = pool_rows(shifted, share, emb_table)
    feature_pos = lax.broadcasted_iota(jnp.int32, (1, features, 1), 1)
    pooled = lax.psum_scatter(
        jnp.where(feature_pos == own_feature, partial_value[:, None, :], 0.0),
        "dev",
        scatter_dimension=0,
        tiled=True,
    )
    id_block = all_ids
    own_ids = lax.dynamic_index_in_dim(id_block, own_feature, 1, keepdims=False)
    shifted, share = relative_ids(own_ids, base_row)
    own_cot = lax.dynamic_index_in_dim(
        lax.all_gather(cotangent, "dev", axis=0, tiled=True), own_feature, 1, keepdims=False
    )
    group_grads = grad_rows(shifted, own_cot * share[:, None], rows_dev)
    row_grads = summed_on_arrival(group_grads, "rep", 0)
    return (pooled, row_grads)


def solution(mesh):
    return jax.shard_map(
        body,
        mesh=mesh,
        in_specs=(
            P("dev", None),
            P(("dev", "rep"), None, None),
            P(("dev", "rep"), None),
            P(("dev", "rep"), None, None),
        ),
        out_specs=(P(("dev", "rep"), None, None), P(("dev", "rep"), None)),
        check_vma=False,
    )
```

profile of v0, /device:TPU:0, one launch (start us, length us, event | category | flops | bytes accessed | tf_op | source)
XLA Modules:
  0.0 340.5 jit_solution(9919795056602686507)
XLA Ops:
  7.2 0.7 all-gather.2.cloned.1.call-update
  7.9 0.7 fusion.77
  8.6 0.9 broadcast_in_dim.49
  9.5 8.3 %all-to-all-start = ((s32[32,128,4,8]{1,3,2,0:T(8,128)}), s32[32,128,4,8]{1,3,2,0:T(8,128)S(1)}, u32[]{:S(2)}, u32[]{:S(2)}) async-start(s32[32,128,4,8]{1,3,2,0:T(8,128)} %broadcast_in_dim.49), calls=%async_computation | async-start | bytes 1048576 | tf_op jit(solution)/shard_map/all_to_all | solution.py:17
  17.9 11.6 %all-to-all-done = s32[32,128,4,8]{1,3,2,0:T(8,128)S(1)} async-done(((s32[32,128,4,8]{1,3,2,0:T(8,128)}), s32[32,128,4,8]{1,3,2,0:T(8,128)S(1)}, u32[]{:S(2)}, u32[]{:S(2)}) %all-to-all-start) | async-done | bytes 524320 | tf_op jit(solution)/shard_map/all_to_all | solution.py:17
  29.6 139.4 %while.25 = (s32[]{:T(128)}, f32[4096,160]{0,1:T(8,128)}, s32[4096,8]{0,1:T(8,128)S(1)}, f32[4096,160]{0,1:T(8,128)}, s32[]{:T(128)}, /*index=5*/s32[]{:T(128)}, s32[]{:T(128)}, s32[]{:T(128)}) while((s32[]{:T(128)}, f32[4096,160]{0,1:T(8,128)}, s32[4096,8]{0,1:T(8,128)S(1)}, f32[4096,160]{0,1:T(8,128)}, s32[]{:T(128)}, ...), condition=%wide.region_1.2_spmd.clone, body=%wide.region_0.1_spmd.clone.sunk | while | flops 8150844416 | bytes 6299805 | solution.py:63
  29.7 34.7 %fusion.104 = f32[4096,160]{0,1:T(8,128)} fusion(s32[1024]{0:T(1024)S(1)} %iota_add_fusion.5, s32[4096]{0:T(1024)S(1)} %bitcast.83, s32[4096]{0:T(1024)S(1)} %bitcast.84, s32[4096]{0:T(1024)S(1)} %bitcast.85, s32[4096]{0:T(1024)S(1)} %bitcast.86, s32[4096]{0:T(1024)S(1)} %bitcast.87, s32[4096]{0:T(1024)S(1)} %bitcast.88, s32[4096]{0:T(1024)S(1)} %bitcast.89, ...), kind=kOutput, calls=%fused_computation.69.clone.1 | convolution fusion | flops 8150843392 | bytes 6033413 | tf_op jit(solution)/shard_map/while/body/eval_jaxpr/dot_general | solution.py:58
  64.5 34.8 %fusion.104 = f32[4096,160]{0,1:T(8,128)} fusion(s32[1024]{0:T(1024)S(1)} %iota_add_fusion.5, s32[4096]{0:T(1024)S(1)} %bitcast.83, s32[4096]{0:T(1024)S(1)} %bitcast.84, s32[4096]{0:T(1024)S(1)} %bitcast.85, s32[4096]{0:T(1024)S(1)} %bitcast.86, s32[4096]{0:T(1024)S(1)} %bitcast.87, s32[4096]{0:T(1024)S(1)} %bitcast.88, s32[4096]{0:T(1024)S(1)} %bitcast.89, ...), kind=kOutput, calls=%fused_computation.69.clone.1 | convolution fusion | flops 8150843392 | bytes 6033413 | tf_op jit(solution)/shard_map/while/body/eval_jaxpr/dot_general | solution.py:58
  99.4 34.8 %fusion.104 = f32[4096,160]{0,1:T(8,128)} fusion(s32[1024]{0:T(1024)S(1)} %iota_add_fusion.5, s32[4096]{0:T(1024)S(1)} %bitcast.83, s32[4096]{0:T(1024)S(1)} %bitcast.84, s32[4096]{0:T(1024)S(1)} %bitcast.85, s32[4096]{0:T(1024)S(1)} %bitcast.86, s32[4096]{0:T(1024)S(1)} %bitcast.87, s32[4096]{0:T(1024)S(1)} %bitcast.88, s32[4096]{0:T(1024)S(1)} %bitcast.89, ...), kind=kOutput, calls=%fused_computation.69.clone.1 | convolution fusion | flops 8150843392 | bytes 6033413 | tf_op jit(solution)/shard_map/while/body/eval_jaxpr/dot_general | solution.py:58
  134.3 34.8 %fusion.104 = f32[4096,160]{0,1:T(8,128)} fusion(s32[1024]{0:T(1024)S(1)} %iota_add_fusion.5, s32[4096]{0:T(1024)S(1)} %bitcast.83, s32[4096]{0:T(1024)S(1)} %bitcast.84, s32[4096]{0:T(1024)S(1)} %bitcast.85, s32[4096]{0:T(1024)S(1)} %bitcast.86, s32[4096]{0:T(1024)S(1)} %bitcast.87, s32[4096]{0:T(1024)S(1)} %bitcast.88, s32[4096]{0:T(1024)S(1)} %bitcast.89, ...), kind=kOutput, calls=%fused_computation.69.clone.1 | convolution fusion | flops 8150843392 | bytes 6033413 | tf_op jit(solution)/shard_map/while/body/eval_jaxpr/dot_general | solution.py:58
  169.0 4.8 %bitcast_multiply_fusion = (f32[4096,160]{0,1:T(8,128)}, f32[4096,160]{0,1:T(8,128)S(1)}) fusion(f32[4096,4,160]{0,2,1:T(8,128)} %all-gather.2.cloned.1.call-done, s32[]{:T(128)S(6)} %select_n.43, f32[4096]{0:T(1024)S(1)} %broadcast_divide_fusion, f32[4096,160]{0,1:T(8,128)} %get-tuple-element.108), kind=kLoop, calls=%fused_computation.74 | loop fusion | flops 1310720 | bytes 10502148 | tf_op jit(solution)/shard_map/mul | solution.py:109
  173.9 5.3 %broadcast_select_fusion = f32[4096,4,160]{0,2,1:T(8,128)} fusion(f32[4096,160]{0,1:T(8,128)S(1)} %get-tuple-element.177, pred[4]{0:T(512)(128)(4,1)S(1)} %iota_compare_fusion.1), kind=kLoop, calls=%fused_computation.73 | loop fusion | flops 2621440 | bytes 13107204 | tf_op jit(solution)/shard_map/jit(_where)/select_n | solution.py:98
  179.2 4.9 %copy.9 = f32[4096,160]{1,0:T(8,128)} copy(f32[4096,160]{0,1:T(8,128)} %get-tuple-element.176) | data formatting | bytes 5242880 | tf_op jit(solution)/shard_map/while | solution.py:77
  184.1 111.3 %while.24 = (s32[]{:T(128)}, f32[4,1024,160]{1,2,0:T(8,128)}, s32[4096,8]{0,1:T(8,128)S(1)}, s32[4]{0:T(128)S(1)}, f32[4096,160]{1,0:T(8,128)}, /*index=5*/s32[]{:T(128)}, s32[1]{0:T(128)}) while((s32[]{:T(128)}, f32[4,1024,160]{1,2,0:T(8,128)}, s32[4096,8]{0,1:T(8,128)S(1)}, s32[4]{0:T(128)S(1)}, f32[4096,160]{1,0:T(8,128)}, ...), condition=%wide.region_5.6_spmd, body=%wide.region_4.5_spmd.sunk | while | flops 8149533696 | bytes 47718544 | solution.py:77
  185.7 13.4 %fusion.99 = f32[4096,1024]{1,0:T(8,128)S(1)} fusion(s32[1024]{0:T(1024)S(1)} %iota_add_fusion.4, s32[4096]{0:T(1024)S(1)} %bitcast.75, s32[4096]{0:T(1024)S(1)} %bitcast.76, s32[4096]{0:T(1024)S(1)} %bitcast.77, s32[4096]{0:T(1024)S(1)} %bitcast.78, s32[4096]{0:T(1024)S(1)} %bitcast.79, s32[4096]{0:T(1024)S(1)} %bitcast.80, ...), kind=kLoop, calls=%fused_computation.1.clone.clone.clone.clone.clone.1.clone.1 | loop fusion | flops 96468992 | bytes 16912384 | tf_op jit(solution)/shard_map/while/body/eval_jaxpr/dot_general | solution.py:73
  199.1 12.7 %fusion.100 = f32[4,1024,160]{1,2,0:T(8,128)} fusion(f32[4,1024,160]{1,2,0:T(8,128)} %get-tuple-element.298, s32[]{:T(128)S(6)} %copy.21, f32[4096,160]{1,0:T(8,128)S(1)} %copy-done, f32[4096,1024]{1,0:T(8,128)S(1)} %fusion.99), kind=kOutput, calls=%fused_computation.34.clone.2 | convolution fusion | flops 8053063680 | bytes 20054020 | tf_op jit(solution)/shard_map/while/body/eval_jaxpr/dot_general | solution.py:73
  213.6 13.4 %fusion.99 = f32[4096,1024]{1,0:T(8,128)S(1)} fusion(s32[1024]{0:T(1024)S(1)} %iota_add_fusion.4, s32[4096]{0:T(1024)S(1)} %bitcast.75, s32[4096]{0:T(1024)S(1)} %bitcast.76, s32[4096]{0:T(1024)S(1)} %bitcast.77, s32[4096]{0:T(1024)S(1)} %bitcast.78, s32[4096]{0:T(1024)S(1)} %bitcast.79, s32[4096]{0:T(1024)S(1)} %bitcast.80, ...), kind=kLoop, calls=%fused_computation.1.clone.clone.clone.clone.clone.1.clone.1 | loop fusion | flops 96468992 | bytes 16912384 | tf_op jit(solution)/shard_map/while/body/eval_jaxpr/dot_general | solution.py:73
  227.1 12.7 %fusion.100 = f32[4,1024,160]{1,2,0:T(8,128)} fusion(f32[4,1024,160]{1,2,0:T(8,128)} %get-tuple-element.298, s32[]{:T(128)S(6)} %copy.21, f32[4096,160]{1,0:T(8,128)S(1)} %copy-done, f32[4096,1024]{1,0:T(8,128)S(1)} %fusion.99), kind=kOutput, calls=%fused_computation.34.clone.2 | convolution fusion | flops 8053063680 | bytes 20054020 | tf_op jit(solution)/shard_map/while/body/eval_jaxpr/dot_general | solution.py:73
  241.4 13.4 %fusion.99 = f32[4096,1024]{1,0:T(8,128)S(1)} fusion(s32[1024]{0:T(1024)S(1)} %iota_add_fusion.4, s32[4096]{0:T(1024)S(1)} %bitcast.75, s32[4096]{0:T(1024)S(1)} %bitcast.76, s32[4096]{0:T(1024)S(1)} %bitcast.77, s32[4096]{0:T(1024)S(1)} %bitcast.78, s32[4096]{0:T(1024)S(1)} %bitcast.79, s32[4096]{0:T(1024)S(1)} %bitcast.80, ...), kind=kLoop, calls=%fused_computation.1.clone.clone.clone.clone.clone.1.clone.1 | loop fusion | flops 96468992 | bytes 16912384 | tf_op jit(solution)/shard_map/while/body/eval_jaxpr/dot_general | solution.py:73
  254.9 12.7 %fusion.100 = f32[4,1024,160]{1,2,0:T(8,128)} fusion(f32[4,1024,160]{1,2,0:T(8,128)} %get-tuple-element.298, s32[]{:T(128)S(6)} %copy.21, f32[4096,160]{1,0:T(8,128)S(1)} %copy-done, f32[4096,1024]{1,0:T(8,128)S(1)} %fusion.99), kind=kOutput, calls=%fused_computation.34.clone.2 | convolution fusion | flops 8053063680 | bytes 20054020 | tf_op jit(solution)/shard_map/while/body/eval_jaxpr/dot_general | solution.py:73
  269.3 13.4 %fusion.99 = f32[4096,1024]{1,0:T(8,128)S(1)} fusion(s32[1024]{0:T(1024)S(1)} %iota_add_fusion.4, s32[4096]{0:T(1024)S(1)} %bitcast.75, s32[4096]{0:T(1024)S(1)} %bitcast.76, s32[4096]{0:T(1024)S(1)} %bitcast.77, s32[4096]{0:T(1024)S(1)} %bitcast.78, s32[4096]{0:T(1024)S(1)} %bitcast.79, s32[4096]{0:T(1024)S(1)} %bitcast.80, ...), kind=kLoop, calls=%fused_computation.1.clone.clone.clone.clone.clone.1.clone.1 | loop fusion | flops 96468992 | bytes 16912384 | tf_op jit(solution)/shard_map/while/body/eval_jaxpr/dot_general | solution.py:73
  282.7 12.7 %fusion.100 = f32[4,1024,160]{1,2,0:T(8,128)} fusion(f32[4,1024,160]{1,2,0:T(8,128)} %get-tuple-element.298, s32[]{:T(128)S(6)} %copy.21, f32[4096,160]{1,0:T(8,128)S(1)} %copy-done, f32[4096,1024]{1,0:T(8,128)S(1)} %fusion.99), kind=kOutput, calls=%fused_computation.34.clone.2 | convolution fusion | flops 8053063680 | bytes 20054020 | tf_op jit(solution)/shard_map/while/body/eval_jaxpr/dot_general | solution.py:73
  295.4 37.1 %all_to_all.10 = f32[4,1024,160]{1,2,0:T(8,128)S(1)} all-to-all(f32[4,1024,160]{1,2,0:T(8,128)} %get-tuple-element.109), channel_id=1, replica_groups=mesh['dev'=32,'rep'=4] {'rep'}, dimensions={0} | all-to-all | bytes 5242880 | tf_op jit(solution)/shard_map/all_to_all | solution.py:32
  332.6 1.1 reduce_sum.20
  (41 shorter events, 3.3 us)
Async XLA Ops:
  7.2 161.9 %all-gather.2.cloned.1.call-start = ((), (), s32[]{:S(2)}) async-start(), calls=%async_computation.4 | async-start | bytes 10813440 | tf_op jit(solution)/shard_map/all_gather | solution.py:107
  9.5 20.0 %all-to-all-start = ((s32[32,128,4,8]{1,3,2,0:T(8,128)}), s32[32,128,4,8]{1,3,2,0:T(8,128)S(1)}, u32[]{:S(2)}, u32[]{:S(2)}) async-start(s32[32,128,4,8]{1,3,2,0:T(8,128)} %broadcast_in_dim.49), calls=%async_computation | async-start | bytes 1048576 | tf_op jit(solution)/shard_map/all_to_all | solution.py:17
  17.8 315.9 %reduce-scatter.2.cloned.1.call-start = ((), (), s32[]{:S(2)}) async-start(), calls=%async_computation.3 | async-start | bytes 10813440 | tf_op jit(solution)/shard_map/reduce_scatter | solution.py:97
  184.1 15.1 %copy-start = (f32[4096,160]{1,0:T(8,128)S(1)}, f32[4096,160]{1,0:T(8,128)}, u32[]{:S(2)}) copy-start(f32[4096,160]{1,0:T(8,128)} %get-tuple-element.308) | copy-start | bytes 7864324 | tf_op jit(solution)/shard_map/while
  211.8 15.2 %copy-start = (f32[4096,160]{1,0:T(8,128)S(1)}, f32[4096,160]{1,0:T(8,128)}, u32[]{:S(2)}) copy-start(f32[4096,160]{1,0:T(8,128)} %get-tuple-element.308) | copy-start | bytes 7864324 | tf_op jit(solution)/shard_map/while
  239.8 15.1 %copy-start = (f32[4096,160]{1,0:T(8,128)S(1)}, f32[4096,160]{1,0:T(8,128)}, u32[]{:S(2)}) copy-start(f32[4096,160]{1,0:T(8,128)} %get-tuple-element.308) | copy-start | bytes 7864324 | tf_op jit(solution)/shard_map/while
  267.6 15.1 %copy-start = (f32[4096,160]{1,0:T(8,128)S(1)}, f32[4096,160]{1,0:T(8,128)}, u32[]{:S(2)}) copy-start(f32[4096,160]{1,0:T(8,128)} %get-tuple-element.308) | copy-start | bytes 7864324 | tf_op jit(solution)/shard_map/while
Sparse Core Ops, SparseCore 0:
  10.1 67.7 all-gather.1
  179.3 97.4 reduce-scatter.1
where the time goes:
time: 341 us; the launch traced here: 340 us
  matrix products  190 us (56%)
  other arithmetic  65.7 us (19%)
  blocking collectives  37.1 us (11%)
  between operations  14.1 us (4%)
  waiting for transfers between devices  12.3 us (4%)
  local copies, waits for them, and re-layouts  8.83 us (3%)
  starting transfers between devices  8.35 us (2%)
  loops' own time  4.24 us (1%)
    dot_general x4, matrix products, add_block(): jnp.dot(counts, table_block, precision=lax.Precision.HIGHEST, preferred_e...  139 us
    dot_general x4, other arithmetic, block_grad(): jnp.dot(counts.T, scaled, precision=lax.Precision.HIGHEST, preferred_elem...  53.6 us
    dot_general x4, matrix products, block_grad(): jnp.dot(counts.T, scaled, precision=lax.Precision.HIGHEST, preferred_elem...  50.8 us
    all_to_all x1, blocking collectives, summed_on_arrival(): pieces = lax.all_to_all(cut_along(x, dim, length), axis, 0, 0, tiled=True)  37.1 us
    all_to_all x1, waiting for transfers between devices, from_everyone(): return lax.all_to_all(copies, axis, split_axis=0, concat_axis=0, tiled=True)  11.6 us
    all_to_all x1, starting transfers between devices, from_everyone(): return lax.all_to_all(copies, axis, split_axis=0, concat_axis=0, tiled=True)  8.27 us
  transfers between devices with their start and end apart: 3, of which 1 were waited for; matrix products, arithmetic and copies ran while one was open for 75% of the time, Pallas kernels for 0%

commit v1 on v0

v1 whole, which is shorter than its diff:
```python
import functools
import jax, jax.numpy as jnp
from jax import lax
from jax.experimental import pallas as pl
from jax.experimental.pallas import tpu as pltpu
from jax.sharding import PartitionSpec as P

LOW = 64
BF = jnp.bfloat16
F32 = jnp.float32


def split_store(dst, cols, x):
    width = x.shape[0]
    high = x.astype(BF)
    dst[0:width, cols] = high
    dst[width : 2 * width, cols] = (x - high.astype(F32)).astype(BF)


def make_keys(base, rows_dev, ids_ref, key_low, key_high, key_count, depth_ref):
    bag = ids_ref.shape[1]
    own, low, valid, lead = [], [], [], []
    for j in range(bag):
        shifted = ids_ref[:, j, :] - base
        good = jnp.logical_and(ids_ref[:, j, :] >= 0, jnp.logical_and(shifted >= 0, shifted < rows_dev))
        own.append(jnp.where(good, shifted, -1))
        low.append(shifted & (LOW - 1))
        valid.append(good)
    deepest = jnp.zeros(own[0].shape, jnp.int32)
    for j in range(bag):
        fresh = valid[j]
        for k in range(j):
            fresh = jnp.logical_and(fresh, own[k] != own[j])
        lead.append(fresh)
    for j in range(bag):
        count = jnp.ones(own[0].shape, F32)
        for k in range(j + 1, bag):
            count = count + jnp.where(own[k] == own[j], 1.0, 0.0)
        level = jnp.zeros(own[0].shape, jnp.int32)
        for k in range(j):
            level = level + jnp.where(jnp.logical_and(lead[k], low[k] == low[j]), 1, 0)
        key_low[j] = jnp.where(lead[j], low[j] + LOW * level, -1)
        key_high[j] = (own[j] >> (LOW.bit_length() - 1)).astype(F32)
        key_count[j] = count
        deepest = jnp.maximum(deepest, jnp.where(lead[j], level + 1, 0))
    depth_ref[0] = jnp.max(deepest)

    @pl.when(depth_ref[0] > 2)
    def _():
        for s in range(deepest.shape[0]):
            depth_ref[1 + s] = jnp.max(deepest[s : s + 1])


def layer_of(source, depth, key_low, key_high, key_count):
    bag = key_low.shape[0]
    place = lax.broadcasted_iota(jnp.int32, (LOW, 128), 0) + LOW * depth
    high = jnp.full((LOW, 128), -1.0, F32)
    count = jnp.zeros((LOW, 128), F32)
    for j in range(bag):
        hit = jnp.broadcast_to(key_low[j, pl.ds(source, 1), :], (LOW, 128)) == place
        high = jnp.where(hit, jnp.broadcast_to(key_high[j, pl.ds(source, 1), :], (LOW, 128)), high)
        count = jnp.where(hit, jnp.broadcast_to(key_count[j, pl.ds(source, 1), :], (LOW, 128)), count)
    return high.astype(BF), count.astype(BF)


def counts_for(block, layers):
    want = jnp.asarray(block, F32).astype(BF)
    tile = jnp.zeros((LOW, 128), BF)
    for high, count in layers:
        tile = jnp.where(high == want, count, tile)
    return tile


def pool_kernel(per_step, base_ref, ids_ref, table_ref, out_ref, highs_ref, counts_ref,
                parts, key_low, key_high, key_count, depth_ref):
    step = pl.program_id(0)
    width, rows_dev = table_ref.shape

    @pl.when(step == 0)
    def _():
        for c in range(0, rows_dev, 512):
            split_store(parts, pl.ds(c, 512), table_ref[:, c : c + 512])
        make_keys(base_ref[0], rows_dev, ids_ref, key_low, key_high, key_count, depth_ref)

    layers = []
    for s in range(per_step):
        source = step * per_step + s
        pair = [layer_of(source, depth, key_low, key_high, key_count) for depth in range(2)]
        for depth in range(2):
            highs_ref[depth, s] = pair[depth][0]
            counts_ref[depth, s] = pair[depth][1]
        layers.append(pair)
    chunk = 512
    total = jnp.zeros((2 * width, 128 * per_step), F32)
    for c in range(0, rows_dev, chunk):
        tile = jnp.concatenate(
            [jnp.concatenate([counts_for(c // LOW + h, layers[s]) for h in range(chunk // LOW)], axis=0)
             for s in range(per_step)], axis=1)
        total = total + jnp.dot(parts[:, c : c + chunk], tile, preferred_element_type=F32)
    for s in range(per_step):
        cols = slice(128 * s, 128 * s + 128)
        out_ref[s] = total[0:width, cols] + total[width : 2 * width, cols]

    @pl.when(depth_ref[0] > 2)
    def _():
        for s in range(per_step):
            source = step * per_step + s

            def deeper(depth, carry):
                extra = layer_of(source, depth, key_low, key_high, key_count)

                def add(block, value):
                    tile = jnp.concatenate(
                        [counts_for(block * (128 // LOW) + h, [extra]) for h in range(128 // LOW)], axis=0)
                    return value + jnp.dot(parts[:, pl.ds(pl.multiple_of(block * 128, 128), 128)],
                                           tile, preferred_element_type=F32)

                more = lax.fori_loop(0, rows_dev // 128, add, jnp.zeros((2 * width, 128), F32))
                out_ref[s] += more[0:width] + more[width : 2 * width]
                return carry

            lax.fori_loop(2, depth_ref[1 + source], deeper, 0)


def pool(base, ids, table_t):
    sources, bag, _ = ids.shape
    width, rows_dev = table_t.shape
    per_step = 2
    full = lambda *shape: pl.BlockSpec(shape, lambda i: (0,) * len(shape))
    return pl.pallas_call(
        functools.partial(pool_kernel, per_step),
        grid=(sources // per_step,),
        in_specs=[pl.BlockSpec(memory_space=pltpu.SMEM), full(sources, bag, 128), full(width, rows_dev)],
        out_specs=[
            pl.BlockSpec((per_step, width, 128), lambda i: (i, 0, 0)),
            pl.BlockSpec((2, per_step, LOW, 128), lambda i: (0, i, 0, 0)),
            pl.BlockSpec((2, per_step, LOW, 128), lambda i: (0, i, 0, 0)),
        ],
        out_shape=[
            jax.ShapeDtypeStruct((sources, width, 128), F32),
            jax.ShapeDtypeStruct((2, sources, LOW, 128), BF),
            jax.ShapeDtypeStruct((2, sources, LOW, 128), BF),
        ],
        scratch_shapes=[
            pltpu.VMEM((2 * width, rows_dev), BF),
            pltpu.VMEM((bag, sources, 128), jnp.int32),
            pltpu.VMEM((bag, sources, 128), F32),
            pltpu.VMEM((bag, sources, 128), F32),
            pltpu.SMEM((1 + sources,), jnp.int32),
        ],
        compiler_params=pltpu.CompilerParams(dimension_semantics=("arbitrary",)),
        name="pool",
    )(base, ids, table_t)


def grad_kernel(first, blk, rows_dev, base_ref, ids_ref, scaled_ref, highs_ref, counts_ref, out_ref,
                parts, key_low, key_high, key_count, depth_ref):
    step = pl.program_id(0)
    sources, width, _ = scaled_ref.shape

    @pl.when(step == 0)
    def _():
        for s in range(sources):
            split_store(parts, pl.ds(128 * s, 128), scaled_ref[s])
        make_keys(base_ref[0], rows_dev, ids_ref, key_low, key_high, key_count, depth_ref)

    start = (first + step) * (blk // LOW)
    together = 4
    total = jnp.zeros((2 * width, blk), F32)
    for s in range(0, sources, together):
        tile = jnp.concatenate(
            [jnp.concatenate([counts_for(start + h, [(highs_ref[d, s + t], counts_ref[d, s + t]) for d in range(2)])
                              for h in range(blk // LOW)], axis=0)
             for t in range(together)], axis=1)
        total = total + lax.dot_general(parts[:, 128 * s : 128 * (s + together)], tile,
                                        (((1,), (1,)), ((), ())), preferred_element_type=F32)
    out_ref[...] = total[0:width] + total[width : 2 * width]

    @pl.when(depth_ref[0] > 2)
    def _():
        def visit(s, carry):
            def deeper(depth, carry):
                extra = layer_of(s, depth, key_low, key_high, key_count)
                tile = jnp.concatenate([counts_for(start + h, [extra]) for h in range(blk // LOW)], axis=0)
                more = lax.dot_general(parts[:, pl.ds(pl.multiple_of(s * 128, 128), 128)], tile,
                                       (((1,), (1,)), ((), ())), preferred_element_type=F32)
                out_ref[...] += more[0:width] + more[width : 2 * width]
                return carry

            return lax.fori_loop(2, depth_ref[1 + s], deeper, carry)

        lax.fori_loop(0, sources, visit, 0)


def grads(base, ids, scaled, highs, counts, rows_dev, groups, first=0, n=16, blk=256):
    sources, bag, _ = ids.shape
    width = scaled.shape[1]
    full = lambda *shape: pl.BlockSpec(shape, lambda i: (0,) * len(shape))
    return pl.pallas_call(
        functools.partial(grad_kernel, first, blk, rows_dev),
        grid=(n,),
        in_specs=[pl.BlockSpec(memory_space=pltpu.SMEM), full(sources, bag, 128), full(sources, width, 128),
                  full(2, sources, LOW, 128), full(2, sources, LOW, 128)],
        out_specs=pl.BlockSpec((None, width, blk), lambda i: (i // (n // groups), 0, i % (n // groups))),
        out_shape=jax.ShapeDtypeStruct((groups, width, n // groups * blk), F32),
        scratch_shapes=[
            pltpu.VMEM((2 * width, sources * 128), BF),
            pltpu.VMEM((bag, sources, 128), jnp.int32),
            pltpu.VMEM((bag, sources, 128), F32),
            pltpu.VMEM((bag, sources, 128), F32),
            pltpu.SMEM((1 + sources,), jnp.int32),
        ],
        compiler_params=pltpu.CompilerParams(dimension_semantics=("arbitrary",)),
        name="grads",
    )(base, ids, scaled, highs, counts)


def to_all(x, axis):
    return lax.all_to_all(x, axis, split_axis=0, concat_axis=0, tiled=True)


def body(emb_table, feature_ids, lengths, cotangent):
    dev_count = lax.axis_size("dev")
    rep_count = lax.axis_size("rep")
    rows_dev, width = emb_table.shape
    examples, features, bag = feature_ids.shape
    owners_each = dev_count // features
    base = (lax.axis_index("dev") % owners_each * rows_dev).astype(jnp.int32).reshape(1)

    ids_t = jnp.transpose(feature_ids, (1, 2, 0))
    share = 1.0 / jnp.transpose(lengths, (1, 0)).astype(F32)
    slot = lax.broadcasted_iota(jnp.int32, ids_t.shape, 1)
    masked = jnp.where(slot < jnp.transpose(lengths, (1, 0))[:, None, :], ids_t, -1)
    ids = to_all(jnp.repeat(masked, owners_each, axis=0), "dev")
    scaled = jnp.transpose(cotangent, (1, 2, 0)) * share[:, None, :]
    scaled_all = to_all(jnp.repeat(scaled, owners_each, axis=0), "dev")
    partial, highs, counts = pool(base, ids, jnp.transpose(emb_table))
    pooled = to_all(partial, "dev").reshape(features, owners_each, width, examples)
    pooled = jnp.sum(pooled, axis=1) * share[:, None, :]
    blocks = grads(base, ids, scaled_all, highs, counts, rows_dev, rep_count)
    row_grads = jnp.sum(to_all(blocks, "rep"), axis=0)
    return jnp.transpose(pooled, (2, 0, 1)), jnp.transpose(row_grads)


def solution(mesh):
    return jax.shard_map(
        body,
        mesh=mesh,
        in_specs=(
            P("dev", None),
            P(("dev", "rep"), None, None),
            P(("dev", "rep"), None),
            P(("dev", "rep"), None, None),
        ),
        out_specs=(P(("dev", "rep"), None, None), P(("dev", "rep"), None)),
        check_vma=False,
    )
```

time: 341 us -> 140 us (0.41)
  matrix products: 190 us -> 0 us
  other arithmetic: 65.7 us -> 6.15 us
  Pallas kernels: 0 us -> 48.8 us
  waiting for transfers between devices: 12.3 us -> 59.1 us
  blocking collectives: 37.1 us -> 0 us
  between operations: 14.1 us -> 0.71 us
  starting transfers between devices: 8.35 us -> 20.9 us
  local copies, waits for them, and re-layouts: 8.83 us -> 3.98 us
  loops' own time: 4.24 us -> 0 us
    dot_general x8 -> x0, matrix products: 190 us -> none  [the longest x4 139 us: add_block(): jnp.dot(counts, table_block, precision=lax.Precision.HIGHEST, preferred_e...]
    dot_general x4 -> x0, other arithmetic: 53.6 us -> none  [block_grad(): jnp.dot(counts.T, scaled, precision=lax.Precision.HIGHEST, preferred_elem...]
    pallas_call x0 -> x2, Pallas kernels: none -> 48.8 us  [the longest x1 26.5 us: grads(): pl.pallas_call(functools.partial(grad_kernel, first, blk, rows_dev), grid...]
    all_to_all x1 -> x4, waiting for transfers between devices: 11.6 us -> 59.1 us  [to_all(): return lax.all_to_all(x, axis, split_axis=0, concat_axis=0, tiled=True)]
    all_to_all x1 -> x0, blocking collectives: 37.1 us -> none  [summed_on_arrival(): pieces = lax.all_to_all(cut_along(x, dim, length), axis, 0, 0, tiled=True)]
    all_to_all x1 -> x4, starting transfers between devices: 8.27 us -> 20.9 us  [to_all(): return lax.all_to_all(x, axis, split_axis=0, concat_axis=0, tiled=True)]
    select_n x3 -> x1, other arithmetic: 6.07 us -> 0.72 us  [body(): jnp.where(slot < jnp.transpose(lengths, (1, 0))[:, None, :], ids_t, -1)]
    while x9 -> x0, local copies, waits for them, and re-layouts: 4.89 us -> none  [the longest x1 4.87 us: grad_rows(): blocks = lax.map(block_grad, jnp.arange(block_count, dtype=jnp.int32))]
  transfers between devices with their start and end apart: 3 -> 4, of which waited for: 1 -> 4; matrix products, arithmetic and copies ran while one was open for 75% -> 2% of each run, Pallas kernels for 0% -> 35%
where the time goes in v1:
time: 140 us
  waiting for transfers between devices  59.1 us (42%)
  Pallas kernels  48.8 us (35%)
  starting transfers between devices  20.9 us (15%)
  other arithmetic  6.15 us (4%)
  local copies, waits for them, and re-layouts  3.98 us (3%)
    all_to_all x4, waiting for transfers between devices, to_all(): return lax.all_to_all(x, axis, split_axis=0, concat_axis=0, tiled=True)  59.1 us
    pallas_call x1, Pallas kernels, grads(): pl.pallas_call(functools.partial(grad_kernel, first, blk, rows_dev), grid...  26.5 us
    pallas_call x1, Pallas kernels, pool(): pl.pallas_call(functools.partial(pool_kernel, per_step), grid=(sources //...  22.4 us
    all_to_all x4, starting transfers between devices, to_all(): return lax.all_to_all(x, axis, split_axis=0, concat_axis=0, tiled=True)  20.9 us
    reduce_sum x1, other arithmetic, body(): row_grads = jnp.sum(to_all(blocks, 'rep'), axis=0)  2.86 us
  transfers between devices with their start and end apart: 4, of which 4 were waited for; matrix products, arithmetic and copies ran while one was open for 2% of the time, Pallas kernels for 35%

profile of v1, /device:TPU:0, one launch (start us, length us, event | category | flops | bytes accessed | tf_op | source)
XLA Modules:
  0.0 139.7 jit_solution(5263285071080358070)
XLA Ops:
  0.6 0.7 bitcast_select_fusion
  1.4 0.7 broadcast_in_dim.14
  2.0 8.3 %all-to-all-start = ((s32[32,8,128]{2,1,0:T(8,128)}), s32[32,8,128]{2,1,0:T(8,128)S(1)}, u32[]{:S(2)}, u32[]{:S(2)}) async-start(s32[32,8,128]{2,1,0:T(8,128)} %bitcast.3), calls=%async_computation | async-start | bytes 262144 | tf_op jit(solution)/shard_map/all_to_all | solution.py:219
  10.3 0.7 convert_divide_fusion
  11.0 1.0 bitcast_multiply_fusion
  12.0 6.1 %all-to-all-done.ids_ref = s32[32,8,128]{2,1,0:T(8,128)S(1)} async-done(((s32[32,8,128]{2,1,0:T(8,128)}), s32[32,8,128]{2,1,0:T(8,128)S(1)}, u32[]{:S(2)}, u32[]{:S(2)}) %all-to-all-start) | async-done | bytes 131104 | tf_op jit(solution)/shard_map/all_to_all | solution.py:219
  18.1 0.0 copy-start.1
  18.1 1.8 %broadcast_in_dim.15 = f32[4,8,160,128]{3,2,1,0:T(8,128)} broadcast(f32[4,160,128]{2,1,0:T(8,128)S(1)} %bitcast_multiply_fusion), dimensions={0,2,3} | broadcast | bytes 2949120 | tf_op jit(solution)/shard_map/broadcast_in_dim | solution.py:236
  19.9 0.0 copy-done.1
  19.9 4.1 %all-to-all-start.2 = ((f32[32,160,128]{2,1,0:T(8,128)}), f32[32,160,128]{2,1,0:T(8,128)S(1)}, u32[]{:S(2)}, u32[]{:S(2)}) async-start(f32[32,160,128]{2,1,0:T(8,128)} %bitcast.8), calls=%async_computation.2 | async-start | bytes 5242880 | tf_op jit(solution)/shard_map/all_to_all | solution.py:219
  24.0 22.4 %pool.1 = (f32[32,160,128]{2,1,0:T(8,128)}, bf16[2,32,64,128]{3,2,1,0:T(8,128)(2,1)}, bf16[2,32,64,128]{3,2,1,0:T(8,128)(2,1)}) custom-call(s32[1]{0:T(128)} %bitcast.base_ref, s32[32,8,128]{2,1,0:T(8,128)} %copy-done.1, f32[160,4096]{1,0:T(8,128)} %bitcast.15), custom_call_target="tpu_custom_call" | custom-call | tf_op jit(solution)/shard_map/pool/pallas_call | solution.py:130
  46.3 13.8 %all-to-all-done.2.scaled_ref = f32[32,160,128]{2,1,0:T(8,128)S(1)} async-done(((f32[32,160,128]{2,1,0:T(8,128)}), f32[32,160,128]{2,1,0:T(8,128)S(1)}, u32[]{:S(2)}, u32[]{:S(2)}) %all-to-all-start.2) | async-done | bytes 2621472 | tf_op jit(solution)/shard_map/all_to_all | solution.py:219
  60.1 0.0 copy-start
  60.1 1.5 %copy-done = f32[32,160,128]{2,1,0:T(8,128)} copy-done((f32[32,160,128]{2,1,0:T(8,128)}, f32[32,160,128]{2,1,0:T(8,128)S(1)}, u32[]{:S(2)}) %copy-start) | copy-done | bytes 2621464
  61.6 4.1 %all-to-all-start.1 = ((f32[32,160,128]{2,1,0:T(8,128)}), f32[32,160,128]{2,1,0:T(8,128)S(1)}, u32[]{:S(2)}, u32[]{:S(2)}) async-start(f32[32,160,128]{2,1,0:T(8,128)} %get-tuple-element.5), calls=%async_computation.1 | async-start | bytes 5242880 | tf_op jit(solution)/shard_map/all_to_all | solution.py:219
  65.7 26.5 %grads.1 = f32[4,160,1024]{2,1,0:T(8,128)} custom-call(s32[1]{0:T(128)} %bitcast.base_ref, s32[32,8,128]{2,1,0:T(8,128)} %copy-done.1, f32[32,160,128]{2,1,0:T(8,128)} %copy-done, bf16[2,32,64,128]{3,2,1,0:T(8,128)(2,1)} %get-tuple-element.6.highs_ref, bf16[2,32,64,128]{3,2,1,0:T(8,128)(2,1)} %get-tuple-element.7.counts_ref), custom_call_target="tpu_custom_call" | custom-call | tf_op jit(solution)/shard_map/grads/pallas_call | solution.py:199
  92.2 0.0 copy-start.2
  92.2 9.7 %all-to-all-done.1 = f32[32,160,128]{2,1,0:T(8,128)S(1)} async-done(((f32[32,160,128]{2,1,0:T(8,128)}), f32[32,160,128]{2,1,0:T(8,128)S(1)}, u32[]{:S(2)}, u32[]{:S(2)}) %all-to-all-start.1) | async-done | bytes 2621472 | tf_op jit(solution)/shard_map/all_to_all | solution.py:219
  101.9 4.5 %all-to-all-start.3 = ((f32[4,160,1024]{2,1,0:T(8,128)}), f32[4,160,1024]{2,1,0:T(8,128)}, u32[]{:S(2)}, u32[]{:S(2)}) async-start(f32[4,160,1024]{2,1,0:T(8,128)} %grads.1), calls=%async_computation.3 | async-start | bytes 5242880 | tf_op jit(solution)/shard_map/all_to_all | solution.py:219
  106.4 0.0 copy-done.2
  106.5 0.1 bitcast_reduce_fusion
  106.6 0.7 bitcast_multiply_fusion.1
  107.3 29.5 %all-to-all-done.3 = f32[4,160,1024]{2,1,0:T(8,128)} async-done(((f32[4,160,1024]{2,1,0:T(8,128)}), f32[4,160,1024]{2,1,0:T(8,128)}, u32[]{:S(2)}, u32[]{:S(2)}) %all-to-all-start.3) | async-done | bytes 2621472 | tf_op jit(solution)/shard_map/all_to_all | solution.py:219
  136.9 2.9 %reduce_sum.22 = f32[160,1024]{1,0:T(8,128)} reduce(f32[4,160,1024]{2,1,0:T(8,128)} %all-to-all-done.3, f32[]{:T(128)} %constant.25.clone.1), dimensions={0}, to_apply=%region_1.2 | reduce | flops 491520 | bytes 3276804 | tf_op jit(solution)/shard_map/reduce_sum | solution.py:241
  (1 shorter events, 0.0 us)
Async XLA Ops:
  2.0 16.1 %all-to-all-start = ((s32[32,8,128]{2,1,0:T(8,128)}), s32[32,8,128]{2,1,0:T(8,128)S(1)}, u32[]{:S(2)}, u32[]{:S(2)}) async-start(s32[32,8,128]{2,1,0:T(8,128)} %bitcast.3), calls=%async_computation | async-start | bytes 262144 | tf_op jit(solution)/shard_map/all_to_all | solution.py:219
  18.1 1.8 %copy-start.1 = (s32[32,8,128]{2,1,0:T(8,128)}, s32[32,8,128]{2,1,0:T(8,128)S(1)}, u32[]{:S(2)}) copy-start(s32[32,8,128]{2,1,0:T(8,128)S(1)} %all-to-all-done.ids_ref) | copy-start | bytes 393220
  19.9 40.3 %all-to-all-start.2 = ((f32[32,160,128]{2,1,0:T(8,128)}), f32[32,160,128]{2,1,0:T(8,128)S(1)}, u32[]{:S(2)}, u32[]{:S(2)}) async-start(f32[32,160,128]{2,1,0:T(8,128)} %bitcast.8), calls=%async_computation.2 | async-start | bytes 5242880 | tf_op jit(solution)/shard_map/all_to_all | solution.py:219
  60.1 1.5 %copy-start = (f32[32,160,128]{2,1,0:T(8,128)}, f32[32,160,128]{2,1,0:T(8,128)S(1)}, u32[]{:S(2)}) copy-start(f32[32,160,128]{2,1,0:T(8,128)S(1)} %all-to-all-done.2.scaled_ref) | copy-start | bytes 7864324
  61.6 40.3 %all-to-all-start.1 = ((f32[32,160,128]{2,1,0:T(8,128)}), f32[32,160,128]{2,1,0:T(8,128)S(1)}, u32[]{:S(2)}, u32[]{:S(2)}) async-start(f32[32,160,128]{2,1,0:T(8,128)} %get-tuple-element.5), calls=%async_computation.1 | async-start | bytes 5242880 | tf_op jit(solution)/shard_map/all_to_all | solution.py:219
  92.2 14.2 %copy-start.2 = (s32[128,4]{0,1:T(4,128)S(1)}, s32[128,4]{0,1:T(4,128)}, u32[]{:S(2)}) copy-start(s32[128,4]{0,1:T(4,128)} %param.6) | copy-start | bytes 6148
  101.9 35.0 %all-to-all-start.3 = ((f32[4,160,1024]{2,1,0:T(8,128)}), f32[4,160,1024]{2,1,0:T(8,128)}, u32[]{:S(2)}, u32[]{:S(2)}) async-start(f32[4,160,1024]{2,1,0:T(8,128)} %grads.1), calls=%async_computation.3 | async-start | bytes 5242880 | tf_op jit(solution)/shard_map/all_to_all | solution.py:219
